TPU v7x, 512 devices: a whole 4x4x16 slice. The times are simulated.
512 devices in a mesh: seq: 64 (over z, x), head: 8 (over y, core).
Axes of the slice: x: 4, y: 4, z: 16, core: 2. Of those that a mesh axis runs over, the one named last changes fastest.
Arguments:
- tokens: bfloat16 [8192, 4096], P('seq', 'head')
- gain: float32 [4096], replicated, may hold values from 0.25 to 1.75
- w_query: bfloat16 [4096, 2048], P('seq', 'head'), may hold values from -0.09375 to 0.09375
- w_key: bfloat16 [4096, 2048], P('seq', 'head'), may hold values from -0.09375 to 0.09375
- w_value: bfloat16 [4096, 2048], P('seq', 'head'), may hold values from -0.09375 to 0.09375
- w_out: bfloat16 [2048, 4096], P('head', 'seq'), may hold values from -0.125 to 0.125
- mem_query: bfloat16 [128, 2048], P(None, 'head'), may hold values from -12 to 12
- score_scale: float32 [16], P('head'), may hold values from 1.5 to 4
- decay: float32 [64, 16], P('seq', 'head'), may hold values from 0 to 1, as said below
- seg_len: int32 [64], P('seq'), may hold values from 32 to 128, as said below
Outputs:
- branch: bfloat16 [8192, 4096], P('seq', 'head')
Inputs may be any that keep to these rules, and one draw needn't show every extreme that they name: `decay`: retention lies strictly between 0 and 1. `seg_len`: at least one segment is full and at least one holds exactly 32 valid tokens.
All inputs are finite; a program needn't handle non-finite values.
Results may differ from a plain program's by a relative error of at most 0.015.
Values may be sent and summed in bfloat16 or wider, within the bound.
A program may use at most 64 MiB of HBM per device.

v0:
```python
import math

import jax
import jax.numpy as jnp
from jax import lax
from jax.sharding import PartitionSpec as P

DH = 128


def carried_in(part, axis, combine, identity):
    place = lax.axis_index(axis)
    gathered = jax.tree.map(lambda a: lax.all_gather(a, axis), part)
    state = jax.tree.map(lambda a, e: jnp.zeros_like(a) + jnp.asarray(e, a.dtype), part, identity)

    def one(lap, state):
        return combine(
            state, jax.tree.map(lambda a: lax.dynamic_index_in_dim(a, lap, 0, False), gathered)
        )

    return lax.fori_loop(0, place, one, state)


def body(tokens, gain, w_query, w_key, w_value, w_out, mem_query, score_scale, decay, seg_len):
    seg_rows, feat_local = tokens.shape
    col_local = w_query.shape[1]
    head_size = DH
    heads_local = col_local // head_size
    slot_count = mem_query.shape[0]
    valid_len = seg_len[0]
    inverse_root_scale = 1.0 / math.sqrt(head_size)
    score_bias = math.log(slot_count + seg_rows)
    whole = lax.all_gather(tokens, "head", axis=1, tiled=True)
    wide = whole.astype(jnp.float32)
    mean_squares = jnp.mean(wide * wide, axis=1, keepdims=True)
    normed = (wide * lax.rsqrt(mean_squares + 1e-05) * gain).astype(jnp.bfloat16)
    pieces = (
        lax.all_gather(w_query, "seq", axis=0, tiled=True),
        lax.all_gather(w_key, "seq", axis=0, tiled=True),
        lax.all_gather(w_value, "seq", axis=0, tiled=True),
    )
    query_sum, key_sum, value_sum = tuple(
        (jnp.dot(normed, piece, preferred_element_type=jnp.float32) for piece in pieces)
    )
    query_head_split = query_sum.astype(jnp.bfloat16).reshape(seg_rows, heads_local, head_size)
    key_head_split = key_sum.astype(jnp.bfloat16).reshape(seg_rows, heads_local, head_size)
    value_head_split = value_sum.astype(jnp.bfloat16).reshape(seg_rows, heads_local, head_size)
    positions = jnp.arange(seg_rows, dtype=jnp.int32)
    valid_keys = (positions < valid_len).astype(jnp.float32)
    memory_head_split = mem_query.reshape(slot_count, heads_local, head_size)
    memory_write_scores = (
        jnp.einsum(
            "bia,sia->ibs", memory_head_split, key_head_split, preferred_element_type=jnp.float32
        )
        * inverse_root_scale
    )
    memory_write_weights = (
        jax.nn.sigmoid(memory_write_scores - math.log(seg_rows)) * valid_keys[None, None, :]
    ).astype(jnp.bfloat16)
    memory_written_keys = jnp.einsum(
        "elz,zek->lek", memory_write_weights, key_head_split, preferred_element_type=jnp.float32
    )
    memory_written_values = jnp.einsum(
        "elz,zek->lek", memory_write_weights, value_head_split, preferred_element_type=jnp.float32
    )
    written = jnp.stack(
        [
            memory_written_keys.reshape(slot_count, col_local),
            memory_written_values.reshape(slot_count, col_local),
        ]
    )

    def combine_state(earlier, later):
        return (
            earlier[0] * later[0],
            jnp.repeat(later[0], head_size)[None, None, :] * earlier[1] + later[1],
        )

    retain = decay[0]
    identity = (jnp.ones_like(retain), jnp.zeros_like(written))
    _, memory_in = carried_in((retain, written), "seq", combine_state, identity)
    mem_split = memory_in.reshape(2, slot_count, heads_local, head_size)
    memory_unit_rows = (
        mem_split * lax.rsqrt(jnp.mean(jnp.square(mem_split), axis=3, keepdims=True) + 1e-06)
    ).astype(jnp.bfloat16)
    head_scale_factors = (score_scale * inverse_root_scale)[:, None, None]
    memory_score_matrix = (
        jnp.einsum(
            "zul,rul->uzr",
            query_head_split,
            memory_unit_rows[0],
            preferred_element_type=jnp.float32,
        )
        * head_scale_factors
    )
    tok_scores = (
        jnp.einsum(
            "thd,shd->hts", query_head_split, key_head_split, preferred_element_type=jnp.float32
        )
        * head_scale_factors
    )
    allowed = (positions[None, :] <= positions[:, None]).astype(jnp.float32) * valid_keys[None, :]
    memory_attention_weights = jax.nn.sigmoid(memory_score_matrix - score_bias).astype(jnp.bfloat16)
    token_attention_weights = (
        jax.nn.sigmoid(tok_scores - score_bias) * allowed[None, :, :]
    ).astype(jnp.bfloat16)
    attended_output = jnp.einsum(
        "krf,fku->rku",
        memory_attention_weights,
        memory_unit_rows[1],
        preferred_element_type=jnp.float32,
    )
    attended_output = attended_output + jnp.einsum(
        "ymo,oyl->myl",
        token_attention_weights,
        value_head_split,
        preferred_element_type=jnp.float32,
    )
    attended_output = (
        (attended_output * valid_keys[:, None, None])
        .astype(jnp.bfloat16)
        .reshape(seg_rows, col_local)
    )
    partial_rows = jnp.dot(
        attended_output,
        lax.all_gather(w_out, "seq", axis=1, tiled=True),
        preferred_element_type=jnp.float32,
    )
    branch = lax.psum_scatter(
        partial_rows.astype(jnp.bfloat16), "head", scatter_dimension=1, tiled=True
    )
    return branch


def solution(mesh):
    return jax.shard_map(
        body,
        mesh=mesh,
        in_specs=(
            P("seq", "head"),
            P(),
            P("seq", "head"),
            P("seq", "head"),
            P("seq", "head"),
            P("head", "seq"),
            P(None, "head"),
            P("head"),
            P("seq", "head"),
            P("seq"),
        ),
        out_specs=P("seq", "head"),
        check_vma=False,
    )
```

profile of v0, /device:TPU:1, one launch (start us, length us, event | category | flops | bytes accessed | tf_op | source)
XLA Modules:
  0.0 845.7 jit_solution(12068725102322100497)
XLA Ops:
  6.5 0.0 copy-start
  6.5 0.0 all-gather.9.cloned.1.call-start
  6.5 0.7 all-gather.9.cloned.1.call-update
  7.3 0.0 all-gather.11.cloned.1.call-start
  7.3 0.7 all-gather.11.cloned.1.call-update
  8.0 0.0 all-gather.13.cloned.1.call-start
  8.1 0.7 all-gather.13.cloned.1.call-update
  8.7 0.0 all-gather.15.cloned.1.call-start
  8.8 0.5 all-gather.15.cloned.1.call-update
  9.3 0.0 all-gather.19.cloned.1.call-start
  10.0 36.3 %all-gather.9.cloned.1.call-done = bf16[128,4096]{1,0:T(8,128)(2,1)} async-done(((bf16[128,512]{1,0:T(8,128)(2,1)}), bf16[128,4096]{1,0:T(8,128)(2,1)}) %all-gather.9.cloned.1.call-update) | async-done | bytes 1048592 | tf_op jit(solution)/shard_map/all_gather | solution.py:33
  46.3 1.5 fusion
  47.8 0.0 copy-start.1
  47.8 0.0 copy-start.3
  47.8 132.0 %all-gather.11.cloned.1.call-done = bf16[4096,256]{1,0:T(8,128)(2,1)} async-done(((bf16[64,256]{1,0:T(8,128)(2,1)}), bf16[4096,256]{1,0:T(8,128)(2,1)}) %all-gather.11.cloned.1.call-update) | async-done | bytes 2097168 | tf_op jit(solution)/shard_map/all_gather | solution.py:39
  179.9 2.4 convolution_convert_fusion.3
  182.3 0.1 copy.33
  182.4 0.0 copy-done
  182.4 0.2 fusion.24
  182.7 0.1 fusion.52
  182.8 0.1 copy.25
  182.9 0.0 copy-start.2
  182.9 0.0 copy-start.4
  182.9 136.8 %all-gather.13.cloned.1.call-done = bf16[4096,256]{1,0:T(8,128)(2,1)} async-done(((bf16[64,256]{1,0:T(8,128)(2,1)}), bf16[4096,256]{1,0:T(8,128)(2,1)}) %all-gather.13.cloned.1.call-update) | async-done | bytes 2097168 | tf_op jit(solution)/shard_map/all_gather | solution.py:40
  319.7 0.0 copy-done.1
  319.7 0.0 copy-done.3
  319.7 2.1 convolution_convert_fusion.2
  321.8 0.1 copy.32
  321.9 0.2 fusion.53
  322.1 0.1 copy.26
  322.2 0.7 pad_maximum_fusion
  322.9 0.0 all-gather.19.cloned.1.call-update
  323.0 0.0 all-gather.17.cloned.1.call-start
  323.0 0.5 all-gather.17.cloned.1.call-update
  323.5 0.0 reduce-scatter.2.cloned.1.call-start
  323.6 0.0 copy-done.2
  323.6 58.7 %all-gather.1 = f32[64,1,2]{2,1,0:T(1,128)S(1)} all-gather(f32[1,1,2]{2,1,0:T(1,128)S(1)} %bitcast.76), channel_id=1, replica_groups=mesh['seq'=64,'head'=8] {'seq'}, dimensions={0}, use_global_device_ids=true | all-gather | bytes 520 | tf_op jit(solution)/shard_map/all_gather | solution.py:13
  382.3 0.0 copy-done.4
  382.3 77.1 %all-gather.15.cloned.1.call-done = bf16[4096,256]{1,0:T(8,128)(2,1)} async-done(((bf16[64,256]{1,0:T(8,128)(2,1)}), bf16[4096,256]{1,0:T(8,128)(2,1)}) %all-gather.15.cloned.1.call-update) | async-done | bytes 2097168 | tf_op jit(solution)/shard_map/all_gather | solution.py:38
  459.4 2.1 fusion.26
  461.5 198.5 %all-gather.19.cloned.1.call-done = f32[128,128,256]{2,1,0:T(8,128)} async-done(((f32[2,128,256]{2,1,0:T(8,128)}), f32[128,128,256]{2,1,0:T(8,128)}) %all-gather.19.cloned.1.call-update) | async-done | bytes 16777232 | tf_op jit(solution)/shard_map/all_gather | solution.py:13
  660.1 0.1 copy.28
  660.3 0.3 fusion.25
  660.6 0.4 fusion.21
  661.0 130.2 %all-gather.17.cloned.1.call-done = bf16[256,4096]{0,1:T(8,128)(2,1)} async-done(((bf16[256,64]{0,1:T(8,128)(2,1)}), bf16[256,4096]{0,1:T(8,128)(2,1)}) %all-gather.17.cloned.1.call-update) | async-done | bytes 2097168 | tf_op jit(solution)/shard_map/all_gather | solution.py:126
  791.1 3.4 convolution_convert_fusion
  794.5 0.0 reduce-scatter.2.cloned.1.call-update
  794.6 44.3 %reduce-scatter.2.cloned.1.call-done = bf16[128,512]{1,0:T(8,128)(2,1)} async-done(((bf16[128,4096]{1,0:T(8,128)(2,1)}), bf16[128,512]{1,0:T(8,128)(2,1)}) %reduce-scatter.2.cloned.1.call-update) | async-done | bytes 131088 | tf_op jit(solution)/shard_map/reduce_scatter | solution.py:129
  (9 shorter events, 0.1 us)
Async XLA Ops:
  6.5 175.9 %copy-start = (bf16[128,256]{1,0:T(8,128)(2,1)S(1)}, bf16[128,256]{1,0:T(8,128)(2,1)}, u32[]{:S(2)}) copy-start(bf16[128,256]{1,0:T(8,128)(2,1)} %param.18) | copy-start | bytes 196612
  6.5 39.8 %all-gather.9.cloned.1.call-start = ((), (), s32[]{:S(2)}) async-start(), calls=%async_computation.1 | async-start | bytes 1179648 | tf_op jit(solution)/shard_map/all_gather | solution.py:33
  7.3 172.6 %all-gather.11.cloned.1.call-start = ((), (), s32[]{:S(2)}) async-start(), calls=%async_computation.2 | async-start | bytes 2129920 | tf_op jit(solution)/shard_map/all_gather | solution.py:39
  8.0 311.7 %all-gather.13.cloned.1.call-start = ((), (), s32[]{:S(2)}) async-start(), calls=%async_computation.3 | async-start | bytes 2129920 | tf_op jit(solution)/shard_map/all_gather | solution.py:40
  8.7 450.6 %all-gather.15.cloned.1.call-start = ((), (), s32[]{:S(2)}) async-start(), calls=%async_computation.4 | async-start | bytes 2129920 | tf_op jit(solution)/shard_map/all_gather | solution.py:38
  9.3 650.7 %all-gather.19.cloned.1.call-start = ((), (), s32[]{:S(2)}) async-start(), calls=%async_computation.7 | async-start | bytes 17039360 | tf_op jit(solution)/shard_map/all_gather | solution.py:13
  47.8 271.9 %copy-start.1 = (bf16[128,4096]{1,0:T(8,128)(2,1)S(1)}, bf16[128,4096]{1,0:T(8,128)(2,1)}, u32[]{:S(2)}) copy-start(bf16[128,4096]{1,0:T(8,128)(2,1)} %all-gather.9.cloned.1.call-done) | copy-start | bytes 3145732
  47.8 271.9 %copy-start.3 = (f32[4096]{0:T(1024)S(1)}, f32[4096]{0:T(1024)}, u32[]{:S(2)}) copy-start(f32[4096]{0:T(1024)} %param.13) | copy-start | bytes 49156
  182.9 140.7 %copy-start.2 = (f32[1,2]{1,0:T(1,128)S(1)}, f32[1,2]{1,0:T(1,128)}, u32[]{:S(2)}) copy-start(f32[1,2]{1,0:T(1,128)} %param.20) | copy-start | bytes 28
  182.9 199.4 %copy-start.4 = (f32[2]{0:T(128)S(1)}, f32[2]{0:T(128)}, u32[]{:S(2)}) copy-start(f32[2]{0:T(128)} %param.19) | copy-start | bytes 28
  323.0 468.2 %all-gather.17.cloned.1.call-start = ((), (), s32[]{:S(2)}) async-start(), calls=%async_computation.5 | async-start | bytes 2129920 | tf_op jit(solution)/shard_map/all_gather | solution.py:126
  323.5 515.3 %reduce-scatter.2.cloned.1.call-start = ((), (), s32[]{:S(2)}) async-start(), calls=%async_computation.6 | async-start | bytes 1179648 | tf_op jit(solution)/shard_map/reduce_scatter | solution.py:129
Sparse Core Ops, SparseCore 0:
  9.5 36.7 all-gather.8
  49.2 130.5 all-gather.10
  182.8 136.8 all-gather.12
  322.5 136.8 all-gather.14
  462.2 197.8 all-gather.18
  662.8 128.2 all-gather.16
  794.7 44.0 reduce-scatter.1
where the time goes:
time: 849 us; the launch traced here: 846 us
  waiting for transfers between devices  758 us (89%)
  blocking collectives  58.7 us (7%)
  between operations  14.3 us (2%)
  matrix products  11.3 us (1%)
    all_gather x1, waiting for transfers between devices, carried_in(): gathered = jax.tree.map(lambda a: lax.all_gather(a, axis), part)  199 us
    all_gather x1, waiting for transfers between devices, body(): lax.all_gather(w_value, 'seq', axis=0, tiled=True)  137 us
    all_gather x1, waiting for transfers between devices, body(): lax.all_gather(w_key, 'seq', axis=0, tiled=True)  132 us
    all_gather x1, waiting for transfers between devices, body(): lax.all_gather(w_out, 'seq', axis=1, tiled=True)  130 us
    all_gather x1, waiting for transfers between devices, body(): lax.all_gather(w_query, 'seq', axis=0, tiled=True)  77.1 us
    all_gather x1, blocking collectives, carried_in(): gathered = jax.tree.map(lambda a: lax.all_gather(a, axis), part)  58.7 us
    reduce_scatter x1, waiting for transfers between devices, body(): lax.psum_scatter(partial_rows.astype(jnp.bfloat16), 'head', scatter_dimen...  44.3 us
    all_gather x1, waiting for transfers between devices, body(): whole = lax.all_gather(tokens, 'head', axis=1, tiled=True)  36.3 us
  transfers between devices with their start and end apart: 7, of which 7 were waited for; matrix products, arithmetic and copies ran while one was open for 1% of the time, Pallas kernels for 0%

commit v1 on v0

v1 whole, which is shorter than its diff:
```python
import functools
import math

import jax
import jax.numpy as jnp
from jax import lax
from jax.experimental import pallas as pl
from jax.experimental.pallas import tpu as pltpu
from jax.sharding import PartitionSpec as P

MESH = pl.DeviceIdType.MESH
NX = 4
NC = 2
SEG = 128
DH = 128
ROWS = 64
F32 = jnp.float32
BF16 = jnp.bfloat16


def kernel(
    nz, ny,
    tok, gain, wq, wk, wv, wo, mq, scale, decay, seglen,
    out,
    wqb, wkb, wvb, wob, mqb, tsend, tkb, tgb,
    skv, rkv, sq, rq, sside, rside,
    tb, rb, eb, me, satt, ratt, pp, pr, ps, sb, orx,
    ring_s, ring_r, loc_s, mq_s, mq_r, t1_s, t1_r, t2_s, t2_r, t3_s, t3_r,
    kv_s, kv_r, q_s, q_r, sd_s, sd_r, wx_s, wx_r, wf_s,
    p1_s, p1_r, p2_s, p2_r, at_s, at_r, pa_s, pa_r, pb_s, pb_r,
):
    seq = lax.axis_index("seq")
    head = lax.axis_index("head")
    z, x = lax.div(seq, NX), lax.rem(seq, NX)
    y, c = lax.div(head, NC), lax.rem(head, NC)
    other = 1 - c
    hx, px = lax.div(x, 2), lax.rem(x, 2)
    features = nz * NX * ROWS

    def dev(zz, xx, yy, cc):
        return {"seq": zz * NX + xx, "head": yy * NC + cc}

    def rc(src, dst, ssem, rsem, target):
        return pltpu.make_async_remote_copy(
            src_ref=src, dst_ref=dst, send_sem=ssem, recv_sem=rsem,
            device_id=target, device_id_type=MESH,
        )

    zr, zl = lax.rem(z + 1, nz), lax.rem(z + nz - 1, nz)
    xs = [lax.rem(x + i, NX) for i in range(NX)]
    ys = [lax.rem(y + i, ny) for i in range(ny)]

    barrier = pltpu.get_barrier_semaphore()
    near = [dev(zr, x, y, c), dev(zl, x, y, c), dev(z, x, y, other)]
    near += [dev(z, xx, y, cc) for xx in xs[1:] for cc in range(NC)]
    near += [dev(z, x, yy, c) for yy in ys[1:]]
    for d in near:
        pl.semaphore_signal(barrier, inc=1, device_id=d, device_id_type=MESH)
    pl.semaphore_wait(barrier, len(near))

    srcs = (wk, wv, wo, wq)

    def slot(a, b):
        if a == 2:
            return wob.at[b, x]
        return (wkb, wvb, None, wqb)[a].at[b]

    def ring(a, way, t):
        step = t - 1
        b = lax.rem(z + nz - step, nz) if way == 0 else lax.rem(z + step, nz)
        first = isinstance(t, int) and t == 1
        return rc(srcs[a] if first else slot(a, b), slot(a, b),
                  ring_s.at[a, way, t], ring_r.at[a, b], dev(zr if way == 0 else zl, x, y, c))

    half = nz // 2

    def long_way(a):
        return a % 2

    def ring_first(a):
        for way in (0, 1):
            ring(a, way, 1).start()

    def ring_mid(arrays, t):
        for a in arrays:
            for way in (0, 1):
                cp = ring(a, way, t)
                cp.wait_recv()
                cp.start()

    def ring_last(arrays):
        for a in arrays:
            for way in (0, 1):
                cp = ring(a, way, half)
                cp.wait_recv()
                if way == long_way(a):
                    cp.start()
        for a in arrays:
            ring(a, long_way(a), half + 1).wait_recv()

    def ring_drain(a):
        for way in (0, 1):
            for t in range(1, half + (1 if way == long_way(a) else 0)):
                ring(a, way, t).wait_send()

    for a in range(4):
        ring_first(a)

    own = [pltpu.make_async_copy(srcs[a], slot(a, z), loc_s.at[a]) for a in range(4)]
    for cp in own:
        cp.start()
    mqc = rc(mq, mqb.at[c], mq_s, mq_r, dev(z, x, y, other))
    mqc.start()

    for i in range(NX):
        tsend[i] = jnp.concatenate(
            [tok[:, 64 * i:64 * i + 64], tok[:, 256 + 64 * i:256 + 64 * i + 64]], axis=1
        )

    def columns(h):
        return pl.ds(pl.multiple_of(h * 128, 128), 128)

    def rows(i):
        return pl.ds(pl.multiple_of(i * 128, 128), 128)

    h_me = y * NC + c

    def t1(i):
        xx = xs[i]
        return rc(tsend.at[xx], tkb.at[rows(x), columns(h_me)], t1_s.at[xx], t1_r.at[x],
                  dev(z, xx, y, c))

    for i in range(1, NX):
        t1(i).start()
    t1_own = pltpu.make_async_copy(tsend.at[x], tkb.at[rows(x), columns(h_me)], loc_s.at[4])
    t1_own.start()

    mid = (0, 1, 2, 3)

    def mid_steps(lo, hi):
        def step(t, carry):
            ring_mid(mid, t)
            return carry
        lax.fori_loop(lo, hi, step, 0)

    cut = min(3, half)
    mid_steps(2, cut)
    t1_own.wait()
    for i in range(1, NX):
        xx = xs[i]
        rc(tsend.at[xx], tkb.at[rows(xx), columns(h_me)], t1_s.at[xx], t1_r.at[xx],
           dev(z, xx, y, c)).wait_recv()

    def t2(i, hh):
        return rc(tkb.at[:, columns(hh)], tkb.at[:, columns(hh)], t2_s.at[i],
                  t2_r.at[lax.div(hh, NC)], dev(z, x, ys[i], c))

    def t3(hh):
        yy = lax.div(hh, NC)
        return rc(tkb.at[:, columns(hh)], tkb.at[:, columns(hh)], t3_s.at[yy], t3_r.at[yy],
                  dev(z, x, y, other))

    for i in range(1, ny):
        t2(i, h_me).start()
    t3(h_me).start()
    cut2 = min(cut + 3, half)
    mid_steps(cut, cut2)
    for i in range(1, ny):
        hh = ys[i] * NC + c
        t2(i, hh).wait_recv()
        t3(hh).start()
    mid_steps(cut2, half)
    ring_last(mid)
    for cp in own:
        cp.wait()

    hz = nz // 2

    def wpart(col, p):
        return wob.at[pl.ds(p * hz, hz), col]

    xr, xm, xl = xs[1], xs[2], xs[3]

    def wx(way, p):
        return rc(wpart(x, p), wpart(x, p), wx_s.at[way, p], wx_r.at[x, p],
                  dev(z, xr if way == 0 else xl, y, c))

    for p in (0, 1):
        wx(0, p).start()
        wx(1, 1 - p).start()

    for i in range(ny):
        hh = ys[i] * NC + other
        rc(tkb.at[:, columns(hh)], tkb.at[:, columns(hh)], t3_s.at[ys[i]], t3_r.at[ys[i]],
           dev(z, x, y, other)).wait_recv()

    ga = gain[pl.ds(hx, ny * NC, stride=4), :]
    gb = gain[pl.ds(2 + hx, ny * NC, stride=4), :]
    even = jnp.concatenate([ga[:, :64], gb[:, :64]], axis=1)
    odd = jnp.concatenate([ga[:, 64:], gb[:, 64:]], axis=1)
    g = jnp.where(px == 0, even, odd)
    ones = jnp.ones((8, 128), BF16)
    ss = jnp.zeros((8, NX * SEG), F32)
    for h in range(ny * NC):
        t = tkb[:, h * 128:h * 128 + 128].astype(F32)
        ss = ss + lax.dot_general(ones, (t * t).astype(BF16), (((1,), (1,)), ((), ())),
                                  preferred_element_type=F32)
        tgb[:, h * 128:h * 128 + 128] = (t * g[h:h + 1, :]).astype(BF16)

    depth = nz * ROWS
    big = tgb[...]
    for a, buf in enumerate((wkb, wvb, wqb)):
        part = jnp.dot(big, buf[...].reshape(depth, 2 * DH), preferred_element_type=F32)
        part = part.astype(BF16)
        for i in range(2):
            for cc in range(NC):
                block = part[cc * 256:cc * 256 + 256, i * DH:i * DH + DH]
                if a < 2:
                    skv[i, cc, :, a * DH:a * DH + DH] = block
                else:
                    sq[i, cc] = block
    row_id = lax.broadcasted_iota(jnp.int32, (8, 256), 0)
    length = seglen[0].astype(F32)
    for i in range(2):
        facts = jnp.where(row_id == 0, decay[0, i], jnp.where(row_id == 1, scale[0, i], length))
        for cc in range(NC):
            sside[i, cc, 0:8] = ss[:, cc * 256:cc * 256 + 256]
            sside[i, cc, 8:16] = facts

    trio = ((sside, rside, sd_s, sd_r), (skv, rkv, kv_s, kv_r), (sq, rq, q_s, q_r))

    def reduce_copy(i, cc, n):
        xx = 2 * c + i
        target = dev(z, xx, y, cc)
        src, dst, ssem, rsem = trio[n]
        return rc(src.at[i, cc], dst.at[x], ssem.at[i, cc], rsem.at[x], target)

    def local_copy(i, cc, n):
        src, dst, ssem, rsem = trio[n]
        return pltpu.make_async_copy(src.at[i, cc], dst.at[x], rsem.at[x])

    for n in range(3):
        for i in range(2):
            for cc in range(NC):
                mine = jnp.logical_and(x == 2 * c + i, c == cc)

                @pl.when(jnp.logical_not(mine))
                def _():
                    reduce_copy(i, cc, n).start()

                @pl.when(mine)
                def _():
                    local_copy(i, cc, n).start()

    def reduce_wait(n, xx):
        target = dev(z, x, y, other)
        src, dst, ssem, rsem = trio[n]
        rc(src.at[0, 0], dst.at[xx], ssem.at[0, 0], rsem.at[xx], target).wait_recv()

    for n in range(2):
        for xx in range(NX):
            reduce_wait(n, xx)

    total = rside[0, 0:8]
    for xx in range(1, NX):
        total = total + rside[xx, 0:8]
    r8 = lax.rsqrt(total * (1.0 / features) + 1e-05)
    kv = rkv[0].astype(F32)
    for xx in range(1, NX):
        kv = kv + rkv[xx].astype(F32)

    rt, keys, values, lens, decays = [], [], [], [], []
    for j in range(2):
        wide = jnp.broadcast_to(r8[0:1, j * 128:j * 128 + 128], (128, 128)).T
        rt.append(wide)
        part = kv[j * 128:j * 128 + 128]
        keys.append((part[:, :DH] * wide).astype(BF16))
        values.append((part[:, DH:] * wide).astype(BF16))
        facts = rside[2 * c + j, 8:16]
        decays.append(facts[0:1, 0:128])
        lens.append(facts[2:3, 0:128])
    score_scale = rside[x, 8:16][1:2, 0:128]

    inverse_root = 1.0 / math.sqrt(DH)
    rc(mq, mqb.at[other], mq_s, mq_r, dev(z, x, y, other)).wait_recv()
    mq_own = mq[:, pl.ds(pl.multiple_of(px * 128, 128), 128)]
    mq_other = mqb[other][:, :].astype(F32)
    mq_other = jnp.where(px == 0, mq_other[:, :DH], mq_other[:, DH:]).astype(BF16)
    mqh = jnp.where(hx == c, mq_own.astype(F32), mq_other.astype(F32)).astype(BF16)

    lane = lax.broadcasted_iota(jnp.int32, (SEG, SEG), 1).astype(F32)
    sub = lax.broadcasted_iota(jnp.int32, (SEG, SEG), 0).astype(F32)
    nt = (((1,), (1,)), ((), ()))
    written = []
    for j in range(2):
        s = lax.dot_general(mqh, keys[j], nt, preferred_element_type=F32) * inverse_root
        w = jax.nn.sigmoid(s - math.log(SEG))
        w = jnp.where(lane < lens[j], w, 0.0).astype(BF16)
        written.append((
            jnp.dot(w, keys[j], preferred_element_type=F32),
            jnp.dot(w, values[j], preferred_element_type=F32),
        ))

    np_ = nz * NC
    per = 2 * SEG // np_
    both = decays[0] * decays[1]
    hi = both.astype(BF16).astype(F32)
    lo = both - hi
    first = lax.broadcasted_iota(jnp.int32, (8, 128), 0) == 0
    dpiece = jnp.where(first, jnp.broadcast_to(hi, (8, 128)), jnp.broadcast_to(lo, (8, 128)))
    for u in range(2):
        t = decays[1] * written[0][u] + written[1][u]
        t = t.reshape(np_ // 2, per, 128)
        d = jnp.broadcast_to(dpiece[None], (np_ // 2, 8, 128))
        tb[u * (np_ // 2):(u + 1) * (np_ // 2)] = jnp.concatenate([t, d], axis=1).astype(BF16)

    g_me = z * NC + c

    def p1(k):
        o = lax.rem(g_me + k, np_)
        return rc(tb.at[o], rb.at[g_me], p1_s.at[k], p1_r.at[g_me],
                  dev(lax.div(o, NC), x, y, lax.rem(o, NC)))

    def p2(k):
        o = lax.rem(g_me + k, np_)
        return rc(eb.at[o], me.at[g_me], p2_s.at[k], p2_r.at[g_me],
                  dev(lax.div(o, NC), x, y, lax.rem(o, NC)))

    def loop(lo_, hi_, f):
        def body(k, carry):
            f(k)
            return carry
        lax.fori_loop(lo_, hi_, body, 0)

    loop(1, np_, lambda k: p1(k).start())
    p1_own = pltpu.make_async_copy(tb.at[g_me], rb.at[g_me], loc_s.at[5])
    p1_own.start()

    def wrelay(way):
        col = xl if way == 0 else xr
        return rc(wpart(col, way), wpart(col, way), wf_s.at[way], wx_r.at[col, way],
                  dev(z, xr if way == 0 else xl, y, c))

    for way in (0, 1):
        cp = wrelay(way)
        cp.wait_recv()
        cp.start()

    for xx in range(NX):
        reduce_wait(2, xx)
    qs = rq[0].astype(F32)
    for xx in range(1, NX):
        qs = qs + rq[xx].astype(F32)
    bias = math.log(SEG + SEG)
    factor = score_scale * inverse_root
    queries, token_part = [], []
    for j in range(2):
        q = (qs[j * 128:j * 128 + 128] * rt[j]).astype(BF16)
        queries.append(q)
        s = lax.dot_general(q, keys[j], nt, preferred_element_type=F32) * factor
        w = jax.nn.sigmoid(s - bias)
        keep = jnp.logical_and(lane <= sub, lane < lens[j])
        w = jnp.where(keep, w, 0.0).astype(BF16)
        token_part.append(jnp.dot(w, values[j], preferred_element_type=F32))

    def p1_arrival(k):
        o = lax.rem(g_me + k, np_)
        rc(tb.at[o], rb.at[o], p1_s.at[k], p1_r.at[o], dev(z, x, y, other)).wait_recv()

    p1_own.wait()
    loop(1, np_, p1_arrival)
    state = jnp.zeros((per, 128), F32)
    for k in range(np_):
        eb[k] = state.astype(BF16)
        piece = rb[k].astype(F32)
        state = (piece[per:per + 1] + piece[per + 1:per + 2]) * state + piece[0:per]
    loop(1, np_, lambda k: p2(k).start())
    p2_own = pltpu.make_async_copy(eb.at[g_me], me.at[g_me], loc_s.at[6])
    p2_own.start()

    def p2_arrival(k):
        o = lax.rem(g_me + k, np_)
        rc(eb.at[o], me.at[o], p2_s.at[k], p2_r.at[o], dev(z, x, y, other)).wait_recv()

    p2_own.wait()
    loop(1, np_, p2_arrival)
    entry = me[...].astype(F32).reshape(2, SEG, DH)

    def unit(m):
        return (m * lax.rsqrt(jnp.mean(m * m, axis=1, keepdims=True) + 1e-06)).astype(BF16)

    for j in range(2):
        if j == 0:
            mem = (entry[0], entry[1])
        else:
            mem = tuple(decays[0] * entry[u] + written[0][u] for u in range(2))
        mk, mv = unit(mem[0]), unit(mem[1])
        s = lax.dot_general(queries[j], mk, nt, preferred_element_type=F32) * factor
        w = jax.nn.sigmoid(s - bias).astype(BF16)
        a = jnp.dot(w, mv, preferred_element_type=F32) + token_part[j]
        satt[j] = jnp.where(sub < lens[j], a, 0.0).astype(BF16)

    def att_copy(j):
        return rc(satt.at[j], ratt.at[:, columns(px)], at_s.at[j], at_r.at[px],
                  dev(z, 2 * c + j, y, hx))

    for j in range(2):
        mine = jnp.logical_and(x == 2 * c + j, c == hx)

        @pl.when(jnp.logical_not(mine))
        def _():
            att_copy(j).start()

        @pl.when(mine)
        def _():
            pltpu.make_async_copy(satt.at[j], ratt.at[:, columns(px)], at_r.at[px]).start()

    for p in (0, 1):
        for col, done in ((xl, 0), (xr, 1)):
            if p != done:
                rc(wpart(col, p), wpart(col, p), wf_s.at[0], wx_r.at[col, p],
                   dev(z, xr, y, c)).wait_recv()
        rc(wpart(xm, p), wpart(xm, p), wf_s.at[0], wx_r.at[xm, p], dev(z, xr, y, c)).wait_recv()

    for j in range(2):
        rc(satt.at[j], ratt.at[:, j * 128:j * 128 + 128], at_s.at[j], at_r.at[j],
           dev(z, x, y, other)).wait_recv()

    att = ratt[...]
    nzs = nz // (ny * NC)

    def wblock(h):
        w = wob[pl.ds(h * nzs, nzs)]
        return w.reshape(nzs * NX * ROWS, 2 * DH)

    def pa(yy):
        return rc(pp.at[yy], pr.at[yy], pa_s.at[yy], pa_r.at[yy], dev(z, x, y, other))

    for yy in range(ny):
        pp[yy] = lax.dot_general(att, wblock(yy * NC + other), nt,
                                 preferred_element_type=F32).astype(BF16)
        pa(yy).start()
    for yy in range(ny):
        ps[yy] = lax.dot_general(att, wblock(yy * NC + c), nt, preferred_element_type=F32)

    def pb(i):
        return rc(sb.at[ys[i]], orx.at[y], pb_s.at[ys[i]], pb_r.at[y], dev(z, x, ys[i], c))

    for yy in range(ny):
        pa(yy).wait_recv()
    for i in list(range(1, ny)):
        sb[ys[i]] = (ps[ys[i]] + pr[ys[i]].astype(F32)).astype(BF16)
        pb(i).start()
    result = ps[y] + pr[y].astype(F32)
    for i in range(1, ny):
        rc(sb.at[ys[i]], orx.at[ys[i]], pb_s.at[ys[i]], pb_r.at[ys[i]],
           dev(z, x, ys[i], c)).wait_recv()
        result = result + orx[ys[i]].astype(F32)
    out[...] = result.astype(BF16)

    for a in range(4):
        ring_drain(a)
    mqc.wait_send()
    for i in range(1, NX):
        t1(i).wait_send()
    for i in range(1, ny):
        t2(i, h_me).wait_send()
    for i in range(ny):
        t3(ys[i] * NC + c).wait_send()
    for way in (0, 1):
        for p in (0, 1):
            wx(way, p).wait_send()
        wrelay(way).wait_send()
    for i in range(2):
        for cc in range(NC):
            mine = jnp.logical_and(x == 2 * c + i, c == cc)

            @pl.when(jnp.logical_not(mine))
            def _():
                for n in range(3):
                    reduce_copy(i, cc, n).wait_send()
    loop(1, np_, lambda k: p1(k).wait_send())
    loop(1, np_, lambda k: p2(k).wait_send())
    for j in range(2):
        mine = jnp.logical_and(x == 2 * c + j, c == hx)

        @pl.when(jnp.logical_not(mine))
        def _():
            att_copy(j).wait_send()
    for yy in range(ny):
        pa(yy).wait_send()
    for i in range(1, ny):
        pb(i).wait_send()


def solution(mesh):
    nz = mesh.shape["seq"] // NX
    ny = mesh.shape["head"] // NC

    def body(tokens, gain, w_query, w_key, w_value, w_out, mem_query, score_scale, decay, seg_len):
        vm = pl.BlockSpec(memory_space=pltpu.VMEM)
        sm = pl.BlockSpec(memory_space=pltpu.SMEM)
        np_ = nz * NC
        per = 2 * SEG // np_
        dma = pltpu.SemaphoreType.DMA
        width = tokens.shape[1]
        scratch = [
            pltpu.VMEM((nz, ROWS, 256), BF16),
            pltpu.VMEM((nz, ROWS, 256), BF16),
            pltpu.VMEM((nz, ROWS, 256), BF16),
            pltpu.VMEM((nz, NX, ROWS, 256), BF16),
            pltpu.VMEM((2, 128, 256), BF16),
            pltpu.VMEM((NX, 128, 128), BF16),
            pltpu.VMEM((NX * SEG, nz * ROWS), BF16),
            pltpu.VMEM((NX * SEG, nz * ROWS), BF16),
            pltpu.VMEM((2, NC, 256, 256), BF16),
            pltpu.VMEM((NX, 256, 256), BF16),
            pltpu.VMEM((2, NC, 256, 128), BF16),
            pltpu.VMEM((NX, 256, 128), BF16),
            pltpu.VMEM((2, NC, 16, 256), F32),
            pltpu.VMEM((NX, 16, 256), F32),
            pltpu.VMEM((np_, per + 8, 128), BF16),
            pltpu.VMEM((np_, per + 8, 128), BF16),
            pltpu.VMEM((np_, per, 128), BF16),
            pltpu.VMEM((np_, per, 128), BF16),
            pltpu.VMEM((2, 128, 128), BF16),
            pltpu.VMEM((128, 256), BF16),
            pltpu.VMEM((ny, 128, width), BF16),
            pltpu.VMEM((ny, 128, width), BF16),
            pltpu.VMEM((ny, 128, width), F32),
            pltpu.VMEM((ny, 128, width), BF16),
            pltpu.VMEM((ny, 128, width), BF16),
            dma((4, 2, nz // 2 + 2)), dma((4, nz)), dma((8,)), dma, dma,
            dma((NX,)), dma((NX,)), dma((ny,)), dma((ny,)), dma((ny,)), dma((ny,)),
            dma((2, 2)), dma((NX,)), dma((2, 2)), dma((NX,)), dma((2, 2)), dma((NX,)),
            dma((2, 2)), dma((NX, 2)), dma((2,)),
            dma((np_,)), dma((np_,)), dma((np_,)), dma((np_,)),
            dma((2,)), dma((2,)), dma((ny,)), dma((ny,)), dma((ny,)), dma((ny,)),
        ]
        return pl.pallas_call(
            functools.partial(kernel, nz, ny),
            out_shape=jax.ShapeDtypeStruct(tokens.shape, BF16),
            in_specs=[vm] * 7 + [sm] * 3,
            out_specs=vm,
            scratch_shapes=scratch,
            compiler_params=pltpu.CompilerParams(
                collective_id=0, has_side_effects=True, vmem_limit_bytes=48 * 1024 * 1024
            ),
        )(
            tokens, gain.reshape(-1, 128), w_query, w_key, w_value, w_out.T, mem_query,
            score_scale.reshape(1, 2), decay, seg_len,
        )

    return jax.shard_map(
        body,
        mesh=mesh,
        in_specs=(
            P("seq", "head"), P(None), P("seq", "head"), P("seq", "head"), P("seq", "head"),
            P("head", "seq"), P(None, "head"), P("head"), P("seq", "head"), P("seq"),
        ),
        out_specs=P("seq", "head"),
        check_vma=False,
    )
```

time: 849 us -> 103 us (0.12)
  waiting for transfers between devices: 758 us -> 0 us
  Pallas kernels: 0 us -> 95 us
  blocking collectives: 58.7 us -> 0 us
  between operations: 14.3 us -> 0.68 us
  matrix products: 11.3 us -> 0 us
    all_gather x6 -> x0, waiting for transfers between devices: 711 us -> none  [the longest x1 199 us: carried_in(): gathered = jax.tree.map(lambda a: lax.all_gather(a, axis), part)]
    pallas_call x0 -> x1, Pallas kernels: none -> 95 us  [body(): pl.pallas_call(functools.partial(kernel, nz, ny), out_shape=jax.ShapeDtyp...]
    all_gather x1 -> x0, blocking collectives: 58.7 us -> none  [carried_in(): gathered = jax.tree.map(lambda a: lax.all_gather(a, axis), part)]
    reduce_scatter x1 -> x0, waiting for transfers between devices: 44.3 us -> none  [body(): lax.psum_scatter(partial_rows.astype(jnp.bfloat16), 'head', scatter_dimen...]
    dot_general x9 -> x0, matrix products: 11.3 us -> none  [the longest x3 6.64 us: body(): jnp.dot(normed, piece, preferred_element_type=jnp.float32)]
  transfers between devices with their start and end apart: 7 -> 0, of which waited for: 7 -> 0; matrix products, arithmetic and copies ran while one was open for 1% -> 0% of each run, Pallas kernels for 0% -> 0%
where the time goes in v1:
time: 103 us
  Pallas kernels  95 us (92%)
  local copies, waits for them, and re-layouts  6.8 us (7%)
    pallas_call x1, Pallas kernels, body(): pl.pallas_call(functools.partial(kernel, nz, ny), out_shape=jax.ShapeDtyp...  95 us
    unnamed x19, local copies, waits for them, and re-layouts  6.8 us

profile of v1, /device:TPU:1, one launch (start us, length us, event | category | flops | bytes accessed | tf_op | source)
XLA Modules:
  0.0 102.5 jit_solution(2843957155866044778)
XLA Ops:
  0.7 0.0 copy-start.7
  0.7 0.0 copy-start.8
  0.7 0.6 copy-done.7
  1.3 0.0 copy-done.8
  1.3 0.0 copy-start
  1.3 0.9 copy-done
  2.2 0.0 copy-start.1
  2.2 0.8 copy-done.1
  3.1 0.0 copy-start.2
  3.1 0.8 copy-done.2
  3.8 0.0 copy-start.3
  3.8 0.8 copy-done.3
  4.6 0.0 copy-start.4
  4.6 0.8 copy-done.4
  5.3 0.0 copy-start.5
  5.3 0.8 copy-done.5
  6.1 0.0 copy-start.6
  6.1 0.7 copy-done.6
  6.8 95.0 %shard_map.100 = bf16[128,512]{1,0:T(8,128)(2,1)S(1)} custom-call(bf16[128,512]{1,0:T(8,128)(2,1)S(1)} %copy-done, f32[32,128]{1,0:T(8,128)S(1)} %bitcast.4, bf16[64,256]{1,0:T(8,128)(2,1)S(1)} %copy-done.2, bf16[64,256]{1,0:T(8,128)(2,1)S(1)} %copy-done.3, bf16[64,256]{1,0:T(8,128)(2,1)S(1)} %copy-done.4, bf16[64,256]{1,0:T(8,128)(2,1)S(1)} %bitcast.3, ...), custom_call_target="tpu_custom_call" | custom-call | tf_op jit(solution)/shard_map/pallas_call | solution.py:540
  101.9 0.7 copy.13
Async XLA Ops:
  0.7 0.7 copy-start.7
  0.7 0.7 copy-start.8
  1.3 0.9 copy-start
  2.2 0.8 copy-start.1
  3.1 0.8 copy-start.2
  3.8 0.8 copy-start.3
  4.6 0.8 copy-start.4
  5.3 0.8 copy-start.5
  6.1 0.7 copy-start.6

commit v2 on v1

--- a/solution.py
+++ b/solution.py
@@ -20,14 +20,15 @@
 
 def kernel(
     nz, ny,
-    tok, gain, wq, wk, wv, wo, mq, scale, decay, seglen,
+    tok_h, gain_h, wq, wk, wv, wo, mq_h, scale_h, decay_h, seglen_h,
     out,
-    wqb, wkb, wvb, wob, mqb, tsend, tkb, tgb,
+    tok, gain, mq, scale, decay, seglen,
+    wqb, wkb, wvb, wr, ws, wf, mqb, tsend, tkb, tgb,
     skv, rkv, sq, rq, sside, rside,
-    tb, rb, eb, me, satt, ratt, pp, pr, ps, sb, orx,
+    tb, rb, eb, me, satt, ratt, sb, orx,
     ring_s, ring_r, loc_s, mq_s, mq_r, t1_s, t1_r, t2_s, t2_r, t3_s, t3_r,
-    kv_s, kv_r, q_s, q_r, sd_s, sd_r, wx_s, wx_r, wf_s,
-    p1_s, p1_r, p2_s, p2_r, at_s, at_r, pa_s, pa_r, pb_s, pb_r,
+    kv_s, kv_r, q_s, q_r, sd_s, sd_r, sw_s, sw_r, wx_s, wx_r, wf_s,
+    p1_s, p1_r, p2_s, p2_r, at_s, at_r, pb_s, pb_r, in_s,
 ):
     seq = lax.axis_index("seq")
     head = lax.axis_index("head")
@@ -50,6 +51,16 @@
     xs = [lax.rem(x + i, NX) for i in range(NX)]
     ys = [lax.rem(y + i, ny) for i in range(ny)]
 
+    stage = [
+        pltpu.make_async_copy(a, b, in_s.at[n])
+        for n, (a, b) in enumerate((
+            (tok_h, tok), (gain_h, gain), (mq_h, mq), (scale_h, scale), (decay_h, decay),
+            (seglen_h, seglen),
+        ))
+    ]
+    for cp in stage:
+        cp.start()
+
     barrier = pltpu.get_barrier_semaphore()
     near = [dev(zr, x, y, c), dev(zl, x, y, c), dev(z, x, y, other)]
     near += [dev(z, xx, y, cc) for xx in xs[1:] for cc in range(NC)]
@@ -62,7 +73,7 @@
 
     def slot(a, b):
         if a == 2:
-            return wob.at[b, x]
+            return wr.at[lax.div(b, 2 * NC), lax.rem(lax.div(b, 2), NC), lax.rem(b, 2)]
         return (wkb, wvb, None, wqb)[a].at[b]
 
     def ring(a, way, t):
@@ -103,15 +114,15 @@
             for t in range(1, half + (1 if way == long_way(a) else 0)):
                 ring(a, way, t).wait_send()
 
-    for a in range(4):
+    early = (0, 1, 3, 2)
+    for a in early:
         ring_first(a)
 
     own = [pltpu.make_async_copy(srcs[a], slot(a, z), loc_s.at[a]) for a in range(4)]
     for cp in own:
         cp.start()
-    mqc = rc(mq, mqb.at[c], mq_s, mq_r, dev(z, x, y, other))
-    mqc.start()
-
+
+    stage[0].wait()
     for i in range(NX):
         tsend[i] = jnp.concatenate(
             [tok[:, 64 * i:64 * i + 64], tok[:, 256 + 64 * i:256 + 64 * i + 64]], axis=1
@@ -135,16 +146,21 @@
     t1_own = pltpu.make_async_copy(tsend.at[x], tkb.at[rows(x), columns(h_me)], loc_s.at[4])
     t1_own.start()
 
-    mid = (0, 1, 2, 3)
-
-    def mid_steps(lo, hi):
-        def step(t, carry):
-            ring_mid(mid, t)
-            return carry
-        lax.fori_loop(lo, hi, step, 0)
-
-    cut = min(3, half)
-    mid_steps(2, cut)
+    stage[2].wait()
+    mqc = rc(mq, mqb.at[c], mq_s, mq_r, dev(z, x, y, other))
+    mqc.start()
+
+    steps = list(range(2, half)) + [half]
+
+    def advance(n):
+        for t in steps[:n]:
+            if t < half:
+                ring_mid(early, t)
+            else:
+                ring_last(early)
+        del steps[:n]
+
+    advance(1)
     t1_own.wait()
     for i in range(1, NX):
         xx = xs[i]
@@ -163,54 +179,55 @@
     for i in range(1, ny):
         t2(i, h_me).start()
     t3(h_me).start()
-    cut2 = min(cut + 3, half)
-    mid_steps(cut, cut2)
+    advance(2)
     for i in range(1, ny):
         hh = ys[i] * NC + c
         t2(i, hh).wait_recv()
         t3(hh).start()
-    mid_steps(cut2, half)
-    ring_last(mid)
-    for cp in own:
-        cp.wait()
-
-    hz = nz // 2
-
-    def wpart(col, p):
-        return wob.at[pl.ds(p * hz, hz), col]
-
-    xr, xm, xl = xs[1], xs[2], xs[3]
-
-    def wx(way, p):
-        return rc(wpart(x, p), wpart(x, p), wx_s.at[way, p], wx_r.at[x, p],
-                  dev(z, xr if way == 0 else xl, y, c))
-
-    for p in (0, 1):
-        wx(0, p).start()
-        wx(1, 1 - p).start()
-
-    for i in range(ny):
-        hh = ys[i] * NC + other
-        rc(tkb.at[:, columns(hh)], tkb.at[:, columns(hh)], t3_s.at[ys[i]], t3_r.at[ys[i]],
-           dev(z, x, y, other)).wait_recv()
-
+    stage[1].wait()
     ga = gain[pl.ds(hx, ny * NC, stride=4), :]
     gb = gain[pl.ds(2 + hx, ny * NC, stride=4), :]
     even = jnp.concatenate([ga[:, :64], gb[:, :64]], axis=1)
     odd = jnp.concatenate([ga[:, 64:], gb[:, 64:]], axis=1)
     g = jnp.where(px == 0, even, odd)
     ones = jnp.ones((8, 128), BF16)
+
+    def stats(h, ss):
+        t = tkb[:, h * 128:h * 128 + 128].astype(F32)
+        tgb[:, h * 128:h * 128 + 128] = (t * g[h:h + 1, :]).astype(BF16)
+        return ss + lax.dot_general(ones, (t * t).astype(BF16), (((1,), (1,)), ((), ())),
+                                    preferred_element_type=F32)
+
+    advance(2)
+    for i in range(ny):
+        hh = ys[i] * NC + other
+        rc(tkb.at[:, columns(hh)], tkb.at[:, columns(hh)], t3_s.at[ys[i]], t3_r.at[ys[i]],
+           dev(z, x, y, other)).wait_recv()
     ss = jnp.zeros((8, NX * SEG), F32)
-    for h in range(ny * NC):
-        t = tkb[:, h * 128:h * 128 + 128].astype(F32)
-        ss = ss + lax.dot_general(ones, (t * t).astype(BF16), (((1,), (1,)), ((), ())),
-                                  preferred_element_type=F32)
-        tgb[:, h * 128:h * 128 + 128] = (t * g[h:h + 1, :]).astype(BF16)
+    for h in range(ny):
+        ss = stats(h, ss)
+    advance(1)
+    for h in range(ny, ny * NC):
+        ss = stats(h, ss)
+    advance(len(steps))
+    for cp in own:
+        cp.wait()
+
+    wmine = wr.at[:, c]
+    swap = rc(wr.at[:, other], ws, sw_s, sw_r, dev(z, x, y, other))
+    swap.start()
+    xr, xm, xl = xs[1], xs[2], xs[3]
+
+    def wx(way, p):
+        return rc(wmine if p == 0 else ws, wf.at[p, x], wx_s.at[way, p], wx_r.at[p, x],
+                  dev(z, xr if way == 0 else xl, y, c))
+
+    wx_own = [pltpu.make_async_copy(wmine if p == 0 else ws, wf.at[p, x], loc_s.at[7 + p])
+              for p in (0, 1)]
 
     depth = nz * ROWS
-    big = tgb[...]
-    for a, buf in enumerate((wkb, wvb, wqb)):
-        part = jnp.dot(big, buf[...].reshape(depth, 2 * DH), preferred_element_type=F32)
+    def project(a, buf):
+        part = jnp.dot(tgb[...], buf[...].reshape(depth, 2 * DH), preferred_element_type=F32)
         part = part.astype(BF16)
         for i in range(2):
             for cc in range(NC):
@@ -219,6 +236,9 @@
                     skv[i, cc, :, a * DH:a * DH + DH] = block
                 else:
                     sq[i, cc] = block
+
+    for cp in stage[3:]:
+        cp.wait()
     row_id = lax.broadcasted_iota(jnp.int32, (8, 256), 0)
     length = seglen[0].astype(F32)
     for i in range(2):
@@ -239,7 +259,7 @@
         src, dst, ssem, rsem = trio[n]
         return pltpu.make_async_copy(src.at[i, cc], dst.at[x], rsem.at[x])
 
-    for n in range(3):
+    def reduce_start(n):
         for i in range(2):
             for cc in range(NC):
                 mine = jnp.logical_and(x == 2 * c + i, c == cc)
@@ -251,6 +271,13 @@
                 @pl.when(mine)
                 def _():
                     local_copy(i, cc, n).start()
+
+    reduce_start(0)
+    project(0, wkb)
+    project(1, wvb)
+    reduce_start(1)
+    project(2, wqb)
+    reduce_start(2)
 
     def reduce_wait(n, xx):
         target = dev(z, x, y, other)
@@ -260,6 +287,13 @@
     for n in range(2):
         for xx in range(NX):
             reduce_wait(n, xx)
+    for way in (0, 1):
+        wx(way, 0).start()
+    swap.wait_recv()
+    for way in (0, 1):
+        wx(way, 1).start()
+    for cp in wx_own:
+        cp.start()
 
     total = rside[0, 0:8]
     for xx in range(1, NX):
@@ -338,13 +372,9 @@
 
     def wrelay(way):
         col = xl if way == 0 else xr
-        return rc(wpart(col, way), wpart(col, way), wf_s.at[way], wx_r.at[col, way],
+        return rc(wf.at[way, col], wf.at[way, col], wf_s.at[way], wx_r.at[way, col],
                   dev(z, xr if way == 0 else xl, y, c))
 
-    for way in (0, 1):
-        cp = wrelay(way)
-        cp.wait_recv()
-        cp.start()
 
     for xx in range(NX):
         reduce_wait(2, xx)
@@ -363,6 +393,9 @@
         w = jnp.where(keep, w, 0.0).astype(BF16)
         token_part.append(jnp.dot(w, values[j], preferred_element_type=F32))
 
+    wrelay(0).wait_recv()
+    wrelay(0).start()
+
     def p1_arrival(k):
         o = lax.rem(g_me + k, np_)
         rc(tb.at[o], rb.at[o], p1_s.at[k], p1_r.at[o], dev(z, x, y, other)).wait_recv()
@@ -378,6 +411,8 @@
     p2_own = pltpu.make_async_copy(eb.at[g_me], me.at[g_me], loc_s.at[6])
     p2_own.start()
 
+    wrelay(1).wait_recv()
+    wrelay(1).start()
     def p2_arrival(k):
         o = lax.rem(g_me + k, np_)
         rc(eb.at[o], me.at[o], p2_s.at[k], p2_r.at[o], dev(z, x, y, other)).wait_recv()
@@ -400,58 +435,53 @@
         a = jnp.dot(w, mv, preferred_element_type=F32) + token_part[j]
         satt[j] = jnp.where(sub < lens[j], a, 0.0).astype(BF16)
 
-    def att_copy(j):
-        return rc(satt.at[j], ratt.at[:, columns(px)], at_s.at[j], at_r.at[px],
-                  dev(z, 2 * c + j, y, hx))
+    def att_slot(cc):
+        return ratt.at[:, columns(jnp.where(hx == cc, 0, 2) + px)]
+
+    def att_copy(j, cc):
+        return rc(satt.at[j], att_slot(cc), at_s.at[j, cc], at_r.at[x],
+                  dev(z, 2 * c + j, y, cc))
 
     for j in range(2):
-        mine = jnp.logical_and(x == 2 * c + j, c == hx)
-
-        @pl.when(jnp.logical_not(mine))
-        def _():
-            att_copy(j).start()
-
-        @pl.when(mine)
-        def _():
-            pltpu.make_async_copy(satt.at[j], ratt.at[:, columns(px)], at_r.at[px]).start()
+        for cc in range(NC):
+            mine = jnp.logical_and(x == 2 * c + j, c == cc)
+
+            @pl.when(jnp.logical_not(mine))
+            def _():
+                att_copy(j, cc).start()
+
+            @pl.when(mine)
+            def _():
+                pltpu.make_async_copy(satt.at[j], att_slot(cc), at_r.at[x]).start()
 
     for p in (0, 1):
-        for col, done in ((xl, 0), (xr, 1)):
-            if p != done:
-                rc(wpart(col, p), wpart(col, p), wf_s.at[0], wx_r.at[col, p],
-                   dev(z, xr, y, c)).wait_recv()
-        rc(wpart(xm, p), wpart(xm, p), wf_s.at[0], wx_r.at[xm, p], dev(z, xr, y, c)).wait_recv()
-
-    for j in range(2):
-        rc(satt.at[j], ratt.at[:, j * 128:j * 128 + 128], at_s.at[j], at_r.at[j],
+        late_col = xr if p == 0 else xl
+        for col in (late_col, xm):
+            rc(wf.at[p, col], wf.at[p, col], wf_s.at[0], wx_r.at[p, col],
+               dev(z, xr, y, c)).wait_recv()
+        wx_own[p].wait()
+    for xx in range(NX):
+        rc(satt.at[0], ratt.at[:, 0:128], at_s.at[0, 0], at_r.at[xx],
            dev(z, x, y, other)).wait_recv()
 
-    att = ratt[...]
-    nzs = nz // (ny * NC)
-
-    def wblock(h):
-        w = wob[pl.ds(h * nzs, nzs)]
-        return w.reshape(nzs * NX * ROWS, 2 * DH)
-
-    def pa(yy):
-        return rc(pp.at[yy], pr.at[yy], pa_s.at[yy], pa_r.at[yy], dev(z, x, y, other))
-
-    for yy in range(ny):
-        pp[yy] = lax.dot_general(att, wblock(yy * NC + other), nt,
-                                 preferred_element_type=F32).astype(BF16)
-        pa(yy).start()
-    for yy in range(ny):
-        ps[yy] = lax.dot_general(att, wblock(yy * NC + c), nt, preferred_element_type=F32)
+    att0, att1 = ratt[:, 0:256], ratt[:, 256:512]
+
+    def product(yy):
+        total = jnp.zeros((SEG, 2 * NX * ROWS), F32)
+        for p, a in ((0, att0), (1, att1)):
+            w = jnp.concatenate(
+                [wf[p, xx, yy, u] for u in range(2) for xx in range(NX)], axis=0
+            )
+            total = total + lax.dot_general(a, w, nt, preferred_element_type=F32)
+        return total
 
     def pb(i):
         return rc(sb.at[ys[i]], orx.at[y], pb_s.at[ys[i]], pb_r.at[y], dev(z, x, ys[i], c))
 
-    for yy in range(ny):
-        pa(yy).wait_recv()
-    for i in list(range(1, ny)):
-        sb[ys[i]] = (ps[ys[i]] + pr[ys[i]].astype(F32)).astype(BF16)
+    for i in ([2] if ny > 2 else []) + [i for i in range(1, ny) if i != 2]:
+        sb[ys[i]] = product(ys[i]).astype(BF16)
         pb(i).start()
-    result = ps[y] + pr[y].astype(F32)
+    result = product(y)
     for i in range(1, ny):
         rc(sb.at[ys[i]], orx.at[ys[i]], pb_s.at[ys[i]], pb_r.at[ys[i]],
            dev(z, x, ys[i], c)).wait_recv()
@@ -461,6 +491,7 @@
     for a in range(4):
         ring_drain(a)
     mqc.wait_send()
+    swap.wait_send()
     for i in range(1, NX):
         t1(i).wait_send()
     for i in range(1, ny):
@@ -482,13 +513,12 @@
     loop(1, np_, lambda k: p1(k).wait_send())
     loop(1, np_, lambda k: p2(k).wait_send())
     for j in range(2):
-        mine = jnp.logical_and(x == 2 * c + j, c == hx)
-
-        @pl.when(jnp.logical_not(mine))
-        def _():
-            att_copy(j).wait_send()
-    for yy in range(ny):
-        pa(yy).wait_send()
+        for cc in range(NC):
+            mine = jnp.logical_and(x == 2 * c + j, c == cc)
+
+            @pl.when(jnp.logical_not(mine))
+            def _():
+                att_copy(j, cc).wait_send()
     for i in range(1, ny):
         pb(i).wait_send()
 
@@ -499,16 +529,23 @@
 
     def body(tokens, gain, w_query, w_key, w_value, w_out, mem_query, score_scale, decay, seg_len):
         vm = pl.BlockSpec(memory_space=pltpu.VMEM)
-        sm = pl.BlockSpec(memory_space=pltpu.SMEM)
         np_ = nz * NC
         per = 2 * SEG // np_
         dma = pltpu.SemaphoreType.DMA
         width = tokens.shape[1]
         scratch = [
+            pltpu.VMEM(tokens.shape, BF16),
+            pltpu.VMEM((gain.shape[0] // 128, 128), F32),
+            pltpu.VMEM((128, 256), BF16),
+            pltpu.SMEM((1, 2), F32),
+            pltpu.SMEM((1, 2), F32),
+            pltpu.SMEM((1,), jnp.int32),
             pltpu.VMEM((nz, ROWS, 256), BF16),
             pltpu.VMEM((nz, ROWS, 256), BF16),
             pltpu.VMEM((nz, ROWS, 256), BF16),
-            pltpu.VMEM((nz, NX, ROWS, 256), BF16),
+            pltpu.VMEM((ny, NC, 2, ROWS, 256), BF16),
+            pltpu.VMEM((ny, 2, ROWS, 256), BF16),
+            pltpu.VMEM((2, NX, ny, 2, ROWS, 256), BF16),
             pltpu.VMEM((2, 128, 256), BF16),
             pltpu.VMEM((NX, 128, 128), BF16),
             pltpu.VMEM((NX * SEG, nz * ROWS), BF16),
@@ -524,27 +561,24 @@
             pltpu.VMEM((np_, per, 128), BF16),
             pltpu.VMEM((np_, per, 128), BF16),
             pltpu.VMEM((2, 128, 128), BF16),
-            pltpu.VMEM((128, 256), BF16),
+            pltpu.VMEM((128, 512), BF16),
             pltpu.VMEM((ny, 128, width), BF16),
             pltpu.VMEM((ny, 128, width), BF16),
-            pltpu.VMEM((ny, 128, width), F32),
-            pltpu.VMEM((ny, 128, width), BF16),
-            pltpu.VMEM((ny, 128, width), BF16),
-            dma((4, 2, nz // 2 + 2)), dma((4, nz)), dma((8,)), dma, dma,
+            dma((4, 2, nz // 2 + 2)), dma((4, nz)), dma((9,)), dma, dma,
             dma((NX,)), dma((NX,)), dma((ny,)), dma((ny,)), dma((ny,)), dma((ny,)),
             dma((2, 2)), dma((NX,)), dma((2, 2)), dma((NX,)), dma((2, 2)), dma((NX,)),
-            dma((2, 2)), dma((NX, 2)), dma((2,)),
+            dma, dma, dma((2, 2)), dma((2, NX)), dma((2,)),
             dma((np_,)), dma((np_,)), dma((np_,)), dma((np_,)),
-            dma((2,)), dma((2,)), dma((ny,)), dma((ny,)), dma((ny,)), dma((ny,)),
+            dma((2, 2)), dma((NX,)), dma((ny,)), dma((ny,)), dma((6,)),
         ]
         return pl.pallas_call(
             functools.partial(kernel, nz, ny),
             out_shape=jax.ShapeDtypeStruct(tokens.shape, BF16),
-            in_specs=[vm] * 7 + [sm] * 3,
+            in_specs=[pl.BlockSpec(memory_space=pl.ANY)] * 10,
             out_specs=vm,
             scratch_shapes=scratch,
             compiler_params=pltpu.CompilerParams(
-                collective_id=0, has_side_effects=True, vmem_limit_bytes=48 * 1024 * 1024
+                collective_id=0, has_side_effects=True, vmem_limit_bytes=60 * 1024 * 1024
             ),
         )(
             tokens, gain.reshape(-1, 128), w_query, w_key, w_value, w_out.T, mem_query,

time: 103 us -> 92.8 us (0.901)
  local copies, waits for them, and re-layouts: 6.8 us -> 1.57 us
  Pallas kernels: 95 us -> 90.4 us
    unnamed x19 -> x1, local copies, waits for them, and re-layouts: 6.8 us -> 1.57 us
    pallas_call x1, Pallas kernels: 95 us -> 90.4 us  [body(): pl.pallas_call(functools.partial(kernel, nz, ny), out_shape=jax.ShapeDtyp...]
where the time goes in v2:
time: 92.8 us; the launch traced here: 92.7 us
  Pallas kernels  90.4 us (97%)
  local copies, waits for them, and re-layouts  1.57 us (2%)
    pallas_call x1, Pallas kernels, body(): pl.pallas_call(functools.partial(kernel, nz, ny), out_shape=jax.ShapeDtyp...  90.4 us

profile of v2, /device:TPU:1, one launch (start us, length us, event | category | flops | bytes accessed | tf_op | source)
XLA Modules:
  0.0 92.7 jit_solution(14866045063731785280)
XLA Ops:
  0.7 90.4 %shard_map.100 = bf16[128,512]{1,0:T(8,128)(2,1)} custom-call(bf16[128,512]{1,0:T(8,128)(2,1)} %tok_h.1, f32[32,128]{1,0:T(8,128)} %bitcast.4, bf16[64,256]{1,0:T(8,128)(2,1)} %wq.1, bf16[64,256]{1,0:T(8,128)(2,1)} %wk.1, bf16[64,256]{1,0:T(8,128)(2,1)} %wv.1, bf16[64,256]{1,0:T(8,128)(2,1)} %bitcast.3, bf16[128,256]{1,0:T(8,128)(2,1)} %mq_h.1, ...), custom_call_target="tpu_custom_call" | custom-call | tf_op jit(solution)/shard_map/pallas_call | solution.py:574
  91.1 1.6 %copy.13 = bf16[128,512]{1,0:T(8,128)(2,1)} copy(bf16[128,512]{1,0:T(8,128)(2,1)} %shard_map.100) | data formatting | bytes 262144

commit v3 on v2

--- a/solution.py
+++ b/solution.py
@@ -23,12 +23,12 @@
     tok_h, gain_h, wq, wk, wv, wo, mq_h, scale_h, decay_h, seglen_h,
     out,
     tok, gain, mq, scale, decay, seglen,
-    wqb, wkb, wvb, wr, ws, wf, mqb, tsend, tkb, tgb,
+    wqb, wkb, wvb, wr, wf, mqb, tsend, tkb, tgb,
     skv, rkv, sq, rq, sside, rside,
-    tb, rb, eb, me, satt, ratt, sb, orx,
+    dv, db, tb, rb, eb, me, satt, ratt, sb, orx,
     ring_s, ring_r, loc_s, mq_s, mq_r, t1_s, t1_r, t2_s, t2_r, t3_s, t3_r,
-    kv_s, kv_r, q_s, q_r, sd_s, sd_r, sw_s, sw_r, wx_s, wx_r, wf_s,
-    p1_s, p1_r, p2_s, p2_r, at_s, at_r, pb_s, pb_r, in_s,
+    kv_s, kv_r, q_s, q_r, sd_s, sd_r, wx_s, wx_r,
+    p0_s, p0_r, p1_s, p1_r, p2_s, p2_r, at_s, at_r, pb_s, pb_r, in_s,
 ):
     seq = lax.axis_index("seq")
     head = lax.axis_index("head")
@@ -46,6 +46,12 @@
             src_ref=src, dst_ref=dst, send_sem=ssem, recv_sem=rsem,
             device_id=target, device_id_type=MESH,
         )
+
+    def loop(lo_, hi_, f):
+        def body(k, carry):
+            f(k)
+            return carry
+        lax.fori_loop(lo_, hi_, body, 0)
 
     zr, zl = lax.rem(z + 1, nz), lax.rem(z + nz - 1, nz)
     xs = [lax.rem(x + i, NX) for i in range(NX)]
@@ -76,12 +82,48 @@
             return wr.at[lax.div(b, 2 * NC), lax.rem(lax.div(b, 2), NC), lax.rem(b, 2)]
         return (wkb, wvb, None, wqb)[a].at[b]
 
+    def block(way, t):
+        return lax.rem(z + nz - (t - 1), nz) if way == 0 else lax.rem(z + t - 1, nz)
+
     def ring(a, way, t):
-        step = t - 1
-        b = lax.rem(z + nz - step, nz) if way == 0 else lax.rem(z + step, nz)
-        first = isinstance(t, int) and t == 1
-        return rc(srcs[a] if first else slot(a, b), slot(a, b),
+        b = block(way, t)
+        return rc(srcs[a] if t == 1 else slot(a, b), slot(a, b),
                   ring_s.at[a, way, t], ring_r.at[a, b], dev(zr if way == 0 else zl, x, y, c))
+
+    def spread(b, i, src):
+        to = lax.rem(lax.div(b, 2), NC)
+        yy, u = lax.div(b, 2 * NC), lax.rem(b, 2)
+        r = jnp.where(to == c, 0, 1)
+        target = dev(z, x, y, other) if i == 0 else dev(z, xs[i], y, to)
+        return rc(src, wf.at[r, x, yy, u], wx_s.at[b, i], wx_r.at[r, x, yy * 2 + u], target)
+
+    def spread_start(b, src):
+        for i in range(1, NX):
+            spread(b, i, src).start()
+        yy, u = lax.div(b, 2 * NC), lax.rem(b, 2)
+        mine = lax.rem(lax.div(b, 2), NC) == c
+
+        @pl.when(jnp.logical_not(mine))
+        def _():
+            spread(b, 0, src).start()
+
+        @pl.when(mine)
+        def _():
+            pltpu.make_async_copy(src, wf.at[0, x, yy, u], wx_r.at[0, x, yy * 2 + u]).start()
+
+    def spread_drain(b):
+        src = slot(2, b)
+        for i in range(1, NX):
+            spread(b, i, src).wait_send()
+
+        @pl.when(lax.rem(lax.div(b, 2), NC) != c)
+        def _():
+            spread(b, 0, src).wait_send()
+
+    def spread_arrived(n):
+        r, xx, v = lax.div(n, NX * ny * 2), lax.rem(lax.div(n, ny * 2), NX), lax.rem(n, ny * 2)
+        ref = wf.at[r, xx, lax.div(v, 2), lax.rem(v, 2)]
+        rc(ref, ref, wx_s.at[0, 0], wx_r.at[r, xx, v], dev(z, x, y, other)).wait_recv()
 
     half = nz // 2
 
@@ -98,6 +140,8 @@
                 cp = ring(a, way, t)
                 cp.wait_recv()
                 cp.start()
+                if a == 2:
+                    spread_start(block(way, t), slot(2, block(way, t)))
 
     def ring_last(arrays):
         for a in arrays:
@@ -106,8 +150,13 @@
                 cp.wait_recv()
                 if way == long_way(a):
                     cp.start()
+                if a == 2:
+                    spread_start(block(way, half), slot(2, block(way, half)))
         for a in arrays:
-            ring(a, long_way(a), half + 1).wait_recv()
+            way = long_way(a)
+            ring(a, way, half + 1).wait_recv()
+            if a == 2:
+                spread_start(block(way, half + 1), slot(2, block(way, half + 1)))
 
     def ring_drain(a):
         for way in (0, 1):
@@ -118,7 +167,8 @@
     for a in early:
         ring_first(a)
 
-    own = [pltpu.make_async_copy(srcs[a], slot(a, z), loc_s.at[a]) for a in range(4)]
+    spread_start(z, srcs[2])
+    own = [pltpu.make_async_copy(srcs[a], slot(a, z), loc_s.at[a]) for a in (0, 1, 3)]
     for cp in own:
         cp.start()
 
@@ -213,18 +263,6 @@
     for cp in own:
         cp.wait()
 
-    wmine = wr.at[:, c]
-    swap = rc(wr.at[:, other], ws, sw_s, sw_r, dev(z, x, y, other))
-    swap.start()
-    xr, xm, xl = xs[1], xs[2], xs[3]
-
-    def wx(way, p):
-        return rc(wmine if p == 0 else ws, wf.at[p, x], wx_s.at[way, p], wx_r.at[p, x],
-                  dev(z, xr if way == 0 else xl, y, c))
-
-    wx_own = [pltpu.make_async_copy(wmine if p == 0 else ws, wf.at[p, x], loc_s.at[7 + p])
-              for p in (0, 1)]
-
     depth = nz * ROWS
     def project(a, buf):
         part = jnp.dot(tgb[...], buf[...].reshape(depth, 2 * DH), preferred_element_type=F32)
@@ -284,17 +322,26 @@
         src, dst, ssem, rsem = trio[n]
         rc(src.at[0, 0], dst.at[xx], ssem.at[0, 0], rsem.at[xx], target).wait_recv()
 
-    for n in range(2):
-        for xx in range(NX):
-            reduce_wait(n, xx)
-    for way in (0, 1):
-        wx(way, 0).start()
-    swap.wait_recv()
-    for way in (0, 1):
-        wx(way, 1).start()
-    for cp in wx_own:
-        cp.start()
-
+    for xx in range(NX):
+        reduce_wait(0, xx)
+
+    np_ = nz * NC
+    g_me = z * NC + c
+
+    def owner(k):
+        o = lax.rem(g_me + k, np_)
+        return o, dev(lax.div(o, NC), x, y, lax.rem(o, NC))
+
+    def p0(k):
+        return rc(dv, db.at[g_me], p0_s.at[k], p0_r.at[g_me], owner(k)[1])
+
+    both = rside[2 * c, 8:16][0:1, 0:128] * rside[2 * c + 1, 8:16][0:1, 0:128]
+    dv[...] = jnp.broadcast_to(both, (8, 128))
+    loop(1, np_, lambda k: p0(k).start())
+    p0_own = pltpu.make_async_copy(dv, db.at[g_me], loc_s.at[4])
+    p0_own.start()
+    for xx in range(NX):
+        reduce_wait(1, xx)
     total = rside[0, 0:8]
     for xx in range(1, NX):
         total = total + rside[xx, 0:8]
@@ -335,46 +382,22 @@
             jnp.dot(w, values[j], preferred_element_type=F32),
         ))
 
-    np_ = nz * NC
     per = 2 * SEG // np_
-    both = decays[0] * decays[1]
-    hi = both.astype(BF16).astype(F32)
-    lo = both - hi
-    first = lax.broadcasted_iota(jnp.int32, (8, 128), 0) == 0
-    dpiece = jnp.where(first, jnp.broadcast_to(hi, (8, 128)), jnp.broadcast_to(lo, (8, 128)))
     for u in range(2):
         t = decays[1] * written[0][u] + written[1][u]
-        t = t.reshape(np_ // 2, per, 128)
-        d = jnp.broadcast_to(dpiece[None], (np_ // 2, 8, 128))
-        tb[u * (np_ // 2):(u + 1) * (np_ // 2)] = jnp.concatenate([t, d], axis=1).astype(BF16)
-
-    g_me = z * NC + c
+        tb[u * (np_ // 2):(u + 1) * (np_ // 2)] = t.reshape(np_ // 2, per, 128).astype(BF16)
 
     def p1(k):
-        o = lax.rem(g_me + k, np_)
-        return rc(tb.at[o], rb.at[g_me], p1_s.at[k], p1_r.at[g_me],
-                  dev(lax.div(o, NC), x, y, lax.rem(o, NC)))
+        o, target = owner(k)
+        return rc(tb.at[o], rb.at[g_me], p1_s.at[k], p1_r.at[g_me], target)
 
     def p2(k):
-        o = lax.rem(g_me + k, np_)
-        return rc(eb.at[o], me.at[g_me], p2_s.at[k], p2_r.at[g_me],
-                  dev(lax.div(o, NC), x, y, lax.rem(o, NC)))
-
-    def loop(lo_, hi_, f):
-        def body(k, carry):
-            f(k)
-            return carry
-        lax.fori_loop(lo_, hi_, body, 0)
+        o, target = owner(k)
+        return rc(eb.at[o], me.at[g_me], p2_s.at[k], p2_r.at[g_me], target)
 
     loop(1, np_, lambda k: p1(k).start())
     p1_own = pltpu.make_async_copy(tb.at[g_me], rb.at[g_me], loc_s.at[5])
     p1_own.start()
-
-    def wrelay(way):
-        col = xl if way == 0 else xr
-        return rc(wf.at[way, col], wf.at[way, col], wf_s.at[way], wx_r.at[way, col],
-                  dev(z, xr if way == 0 else xl, y, c))
-
 
     for xx in range(NX):
         reduce_wait(2, xx)
@@ -393,30 +416,50 @@
         w = jnp.where(keep, w, 0.0).astype(BF16)
         token_part.append(jnp.dot(w, values[j], preferred_element_type=F32))
 
-    wrelay(0).wait_recv()
-    wrelay(0).start()
-
     def p1_arrival(k):
         o = lax.rem(g_me + k, np_)
         rc(tb.at[o], rb.at[o], p1_s.at[k], p1_r.at[o], dev(z, x, y, other)).wait_recv()
 
+    def p0_arrival(k):
+        o = owner(k)[0]
+        rc(dv, db.at[o], p0_s.at[k], p0_r.at[o], dev(z, x, y, other)).wait_recv()
+
+    p0_own.wait()
+    loop(1, np_, p0_arrival)
     p1_own.wait()
     loop(1, np_, p1_arrival)
     state = jnp.zeros((per, 128), F32)
     for k in range(np_):
         eb[k] = state.astype(BF16)
-        piece = rb[k].astype(F32)
-        state = (piece[per:per + 1] + piece[per + 1:per + 2]) * state + piece[0:per]
+        state = db[k][0:1] * state + rb[k].astype(F32)
     loop(1, np_, lambda k: p2(k).start())
     p2_own = pltpu.make_async_copy(eb.at[g_me], me.at[g_me], loc_s.at[6])
     p2_own.start()
 
-    wrelay(1).wait_recv()
-    wrelay(1).start()
     def p2_arrival(k):
         o = lax.rem(g_me + k, np_)
         rc(eb.at[o], me.at[o], p2_s.at[k], p2_r.at[o], dev(z, x, y, other)).wait_recv()
 
+    for a in range(4):
+        ring_drain(a)
+    mqc.wait_send()
+    for i in range(1, NX):
+        t1(i).wait_send()
+    for i in range(1, ny):
+        t2(i, h_me).wait_send()
+    for i in range(ny):
+        t3(ys[i] * NC + c).wait_send()
+    loop(0, nz, spread_drain)
+    for i in range(2):
+        for cc in range(NC):
+            mine = jnp.logical_and(x == 2 * c + i, c == cc)
+
+            @pl.when(jnp.logical_not(mine))
+            def _():
+                for n in range(3):
+                    reduce_copy(i, cc, n).wait_send()
+    loop(1, np_, lambda k: p0(k).wait_send())
+    loop(1, np_, lambda k: p1(k).wait_send())
     p2_own.wait()
     loop(1, np_, p2_arrival)
     entry = me[...].astype(F32).reshape(2, SEG, DH)
@@ -454,15 +497,11 @@
             def _():
                 pltpu.make_async_copy(satt.at[j], att_slot(cc), at_r.at[x]).start()
 
-    for p in (0, 1):
-        late_col = xr if p == 0 else xl
-        for col in (late_col, xm):
-            rc(wf.at[p, col], wf.at[p, col], wf_s.at[0], wx_r.at[p, col],
-               dev(z, xr, y, c)).wait_recv()
-        wx_own[p].wait()
     for xx in range(NX):
         rc(satt.at[0], ratt.at[:, 0:128], at_s.at[0, 0], at_r.at[xx],
            dev(z, x, y, other)).wait_recv()
+
+    loop(0, 2 * NX * ny * 2, spread_arrived)
 
     att0, att1 = ratt[:, 0:256], ratt[:, 256:512]
 
@@ -488,29 +527,6 @@
         result = result + orx[ys[i]].astype(F32)
     out[...] = result.astype(BF16)
 
-    for a in range(4):
-        ring_drain(a)
-    mqc.wait_send()
-    swap.wait_send()
-    for i in range(1, NX):
-        t1(i).wait_send()
-    for i in range(1, ny):
-        t2(i, h_me).wait_send()
-    for i in range(ny):
-        t3(ys[i] * NC + c).wait_send()
-    for way in (0, 1):
-        for p in (0, 1):
-            wx(way, p).wait_send()
-        wrelay(way).wait_send()
-    for i in range(2):
-        for cc in range(NC):
-            mine = jnp.logical_and(x == 2 * c + i, c == cc)
-
-            @pl.when(jnp.logical_not(mine))
-            def _():
-                for n in range(3):
-                    reduce_copy(i, cc, n).wait_send()
-    loop(1, np_, lambda k: p1(k).wait_send())
     loop(1, np_, lambda k: p2(k).wait_send())
     for j in range(2):
         for cc in range(NC):
@@ -544,7 +560,6 @@
             pltpu.VMEM((nz, ROWS, 256), BF16),
             pltpu.VMEM((nz, ROWS, 256), BF16),
             pltpu.VMEM((ny, NC, 2, ROWS, 256), BF16),
-            pltpu.VMEM((ny, 2, ROWS, 256), BF16),
             pltpu.VMEM((2, NX, ny, 2, ROWS, 256), BF16),
             pltpu.VMEM((2, 128, 256), BF16),
             pltpu.VMEM((NX, 128, 128), BF16),
@@ -556,8 +571,10 @@
             pltpu.VMEM((NX, 256, 128), BF16),
             pltpu.VMEM((2, NC, 16, 256), F32),
             pltpu.VMEM((NX, 16, 256), F32),
-            pltpu.VMEM((np_, per + 8, 128), BF16),
-            pltpu.VMEM((np_, per + 8, 128), BF16),
+            pltpu.VMEM((8, 128), F32),
+            pltpu.VMEM((np_, 8, 128), F32),
+            pltpu.VMEM((np_, per, 128), BF16),
+            pltpu.VMEM((np_, per, 128), BF16),
             pltpu.VMEM((np_, per, 128), BF16),
             pltpu.VMEM((np_, per, 128), BF16),
             pltpu.VMEM((2, 128, 128), BF16),
@@ -567,8 +584,8 @@
             dma((4, 2, nz // 2 + 2)), dma((4, nz)), dma((9,)), dma, dma,
             dma((NX,)), dma((NX,)), dma((ny,)), dma((ny,)), dma((ny,)), dma((ny,)),
             dma((2, 2)), dma((NX,)), dma((2, 2)), dma((NX,)), dma((2, 2)), dma((NX,)),
-            dma, dma, dma((2, 2)), dma((2, NX)), dma((2,)),
-            dma((np_,)), dma((np_,)), dma((np_,)), dma((np_,)),
+            dma((nz, NX)), dma((2, NX, ny * 2)),
+            dma((np_,)), dma((np_,)), dma((np_,)), dma((np_,)), dma((np_,)), dma((np_,)),
             dma((2, 2)), dma((NX,)), dma((ny,)), dma((ny,)), dma((6,)),
         ]
         return pl.pallas_call(

time: 92.8 us -> 90.8 us (0.978)
  Pallas kernels: 90.4 us -> 88.4 us
    pallas_call x1, Pallas kernels: 90.4 us -> 88.4 us  [body(): pl.pallas_call(functools.partial(kernel, nz, ny), out_shape=jax.ShapeDtyp...]
where the time goes in v3:
time: 90.8 us; the launch traced here: 90.6 us
  Pallas kernels  88.4 us (97%)
  local copies, waits for them, and re-layouts  1.57 us (2%)
    pallas_call x1, Pallas kernels, body(): pl.pallas_call(functools.partial(kernel, nz, ny), out_shape=jax.ShapeDtyp...  88.4 us

profile of v3, /device:TPU:1, one launch (start us, length us, event | category | flops | bytes accessed | tf_op | source)
XLA Modules:
  0.0 90.6 jit_solution(4578491187950268132)
XLA Ops:
  0.7 88.4 %shard_map.100 = bf16[128,512]{1,0:T(8,128)(2,1)} custom-call(bf16[128,512]{1,0:T(8,128)(2,1)} %tok_h.1, f32[32,128]{1,0:T(8,128)} %bitcast.4, bf16[64,256]{1,0:T(8,128)(2,1)} %wq.1, bf16[64,256]{1,0:T(8,128)(2,1)} %wk.1, bf16[64,256]{1,0:T(8,128)(2,1)} %wv.1, bf16[64,256]{1,0:T(8,128)(2,1)} %bitcast.3, bf16[128,256]{1,0:T(8,128)(2,1)} %mq_h.1, ...), custom_call_target="tpu_custom_call" | custom-call | tf_op jit(solution)/shard_map/pallas_call | solution.py:591
  89.1 1.6 %copy.13 = bf16[128,512]{1,0:T(8,128)(2,1)} copy(bf16[128,512]{1,0:T(8,128)(2,1)} %shard_map.100) | data formatting | bytes 262144
